TPU v7x, 32 devices: a whole 2x2x4 slice. The times are simulated.
32 devices in a mesh: row: 8 (over y, x, core), col: 4 (over z).
Axes of the slice: x: 2, y: 2, z: 4, core: 2. Of those that a mesh axis runs over, the one named last changes fastest.
Arguments:
- attn_out: bfloat16 [2, 256, 16384], P(None, 'row', 'col'), may hold values from -6 to 6
- o_weight: bfloat16 [16384, 16384], P('col', 'row'), may hold values from -0.046875 to 0.046875
- residual: float32 [2, 256, 16384], P(None, 'col', 'row'), may hold values from -73 to 73
- norm_gain: float32 [16384], replicated, may hold values from 0.5 to 1.5
- gram_in: float32 [16384, 16384], P('row', 'col'), may hold values from -0.1 to 1.5
Outputs:
- gram: float32 [16384, 16384], P('row', 'col')
All inputs are finite; a program needn't handle non-finite values.
Results may differ from a plain program's by a relative error of at most 0.0003.
Values may be sent and summed in bfloat16 or wider, within the bound.
A program may use at most 192 MiB of HBM per device.

v0:
```python
import jax
import jax.numpy as jnp
from jax import lax
from jax.sharding import PartitionSpec as P

epsilon_norm = 1e-05
highest = lax.Precision.HIGHEST


def spread(block, axis, owner):
    block = jnp.where(lax.axis_index(axis) == owner, block, jnp.zeros_like(block))
    return lax.psum(block, axis)


def outer_sum(left_rows, right_rows):
    return lax.dot_general(
        left_rows,
        right_rows,
        (((0,), (0,)), ((), ())),
        precision=highest,
        preferred_element_type=jnp.float32,
    )


def body(attn_out, o_weight, residual, norm_gain, gram_in):
    row_count = lax.axis_size("row")
    col_count = lax.axis_size("col")
    fan_ratio = row_count // col_count
    row_index = lax.axis_index("row")
    col_index = lax.axis_index("col")
    col_width = o_weight.shape[0]
    row_width = o_weight.shape[1]
    model_width = row_width * row_count
    group_tokens = attn_out.shape[1] * row_count
    local_tokens = residual.shape[1]
    gain_rows = lax.dynamic_slice_in_dim(norm_gain, row_index * row_width, row_width)
    gram_sum = jnp.zeros((row_width, col_width), jnp.float32)
    for block_index in range(attn_out.shape[0]):
        resid_block = residual[block_index]
        partial_value = jnp.dot(
            lax.all_gather(attn_out[block_index], "row", axis=0, tiled=True),
            o_weight,
            preferred_element_type=jnp.float32,
        )
        offset = col_index * local_tokens
        own_rows = lax.dynamic_slice_in_dim(partial_value, offset, local_tokens, 0) + resid_block
        partial_value = lax.dynamic_update_slice_in_dim(partial_value, own_rows, offset, 0)
        row_panel = lax.psum(partial_value, "col")
        panel_sums = lax.psum(jnp.sum(row_panel * row_panel, axis=1), "row")
        inverse_rms = lax.rsqrt(panel_sums / model_width + epsilon_norm)
        row_panel = row_panel * inverse_rms[:, None] * gain_rows[None, :]
        column_parts = []
        for member in range(fan_ratio):
            column_parts.append(spread(row_panel, "row", col_index * fan_ratio + member))
        column_block = jnp.concatenate(column_parts, axis=1)
        gram_sum = gram_sum + outer_sum(row_panel, column_block)
    return gram_in + gram_sum / (attn_out.shape[0] * group_tokens)


def solution(mesh):
    return jax.shard_map(
        body,
        mesh=mesh,
        in_specs=(
            P(None, "row", "col"),
            P("col", "row"),
            P(None, "col", "row"),
            P(),
            P("row", "col"),
        ),
        out_specs=P("row", "col"),
        check_vma=False,
    )
```

profile of v0, /device:TPU:0, one launch (start us, length us, event | category | flops | bytes accessed | tf_op | source)
XLA Modules:
  0.0 466.1 jit_solution(1088472988798540097)
XLA Ops:
  6.5 0.0 all-gather.7.cloned.1.call-start
  6.5 1.8 fusion.23
  8.4 0.0 all-gather.7.cloned.1.call-update
  8.4 0.0 all-gather.5.cloned.1.call-start
  8.5 0.7 all-gather.5.cloned.1.call-update
  9.2 0.0 all-reduce.8.cloned.1.call-start
  9.2 30.5 %all-gather.7.cloned.1.call-done = bf16[1,256,4096]{2,1,0:T(8,128)(2,1)} async-done(((bf16[1,32,4096]{2,1,0:T(8,128)(2,1)}), bf16[1,256,4096]{2,1,0:T(8,128)(2,1)}) %all-gather.7.cloned.1.call-update) | async-done | bytes 2097168 | tf_op jit(solution)/shard_map/all_gather | solution.py:41
  39.8 8.7 %fusion.7 = f32[256,2048]{1,0:T(8,128)S(1)} fusion(bf16[4096,2048]{1,0:T(8,128)(2,1)} %param.6, bf16[1,256,4096]{2,1,0:T(8,128)(2,1)} %all-gather.7.cloned.1.call-done), kind=kOutput, calls=%fused_computation.8 | convolution fusion | flops 4294967296 | bytes 20971520 | tf_op jit(solution)/shard_map/dot_general | solution.py:40
  48.5 0.0 copy-start.3
  48.5 21.0 %all-gather.5.cloned.1.call-done = bf16[1,256,4096]{2,1,0:T(8,128)(2,1)} async-done(((bf16[1,32,4096]{2,1,0:T(8,128)(2,1)}), bf16[1,256,4096]{2,1,0:T(8,128)(2,1)}) %all-gather.5.cloned.1.call-update) | async-done | bytes 2097168 | tf_op jit(solution)/shard_map/all_gather | solution.py:41
  69.5 8.7 %fusion.9 = f32[256,2048]{1,0:T(8,128)S(1)} fusion(bf16[4096,2048]{1,0:T(8,128)(2,1)} %param.6, bf16[1,256,4096]{2,1,0:T(8,128)(2,1)} %all-gather.5.cloned.1.call-done), kind=kOutput, calls=%fused_computation.10 | convolution fusion | flops 4294967296 | bytes 20971520 | tf_op jit(solution)/shard_map/dot_general | solution.py:40
  78.2 0.0 copy-done.3
  78.2 0.2 fusion.19
  78.4 0.0 copy-start.2
  78.4 1.3 copy-done.2
  79.7 0.0 copy-start.1
  79.7 1.3 copy-done.1
  81.1 0.0 all-reduce.8.cloned.1.call-update
  81.1 0.0 all-reduce.6.cloned.1.call-start
  81.2 0.7 dynamic_slice.10
  81.9 154.4 %all-reduce.8.cloned.1.call-done = (f32[256,2048]{1,0:T(8,128)}, f32[256,2048]{1,0:T(8,128)}) async-done(((f32[256,2048]{1,0:T(8,128)}, f32[256,2048]{1,0:T(8,128)}), (f32[256,2048]{1,0:T(8,128)}, f32[256,2048]{1,0:T(8,128)})) %all-reduce.8.cloned.1.call-update) | async-done | bytes 4194320 | tf_op jit(solution)/shard_map/psum | solution.py:48
  236.3 0.0 copy-start
  236.3 2.7 multiply_reduce_fusion
  239.0 13.6 %all-reduce = (f32[256]{0:T(256)S(1)}, f32[256]{0:T(256)S(1)}) all-reduce(f32[256]{0:T(256)S(1)} %get-tuple-element.24, f32[256]{0:T(256)S(1)} %get-tuple-element.23), channel_id=1, replica_groups=mesh['row'=8,'col'=4] {'row'}, use_global_device_ids=true, to_apply=%region_2.0 | all-reduce | flops 512 | bytes 4096 | tf_op jit(solution)/shard_map/psum | solution.py:49
  252.6 0.0 copy-done
  252.6 5.4 %fusion.14 = (f32[256,2048]{1,0:T(8,128)}, f32[256,2048]{1,0:T(8,128)}, f32[256,2048]{1,0:T(8,128)}, f32[256,2048]{1,0:T(8,128)}) fusion(f32[256,2048]{1,0:T(8,128)} %get-tuple-element.12, f32[256]{0:T(256)S(1)} %add_rsqrt_fusion, f32[2048]{0:T(1024)S(1)} %dynamic_slice.10, pred[]{:T(512)S(6)} %eq.8, pred[]{:T(512)S(6)} %eq.9, f32[256,2048]{1,0:T(8,128)S(1)} %copy-done, ...), kind=kLoop, calls=%fused_computation.19 | loop fusion | flops 4194304 | bytes 12593154 | tf_op jit(solution)/shard_map/jit(_where)/select_n | solution.py:11
  258.1 0.0 all-reduce.6.cloned.1.call-update
  258.1 123.8 %all-reduce.6.cloned.1.call-done = (f32[256,2048]{1,0:T(8,128)}, f32[256,2048]{1,0:T(8,128)}, f32[256,2048]{1,0:T(8,128)}, f32[256,2048]{1,0:T(8,128)}) async-done(((f32[256,2048]{1,0:T(8,128)}, f32[256,2048]{1,0:T(8,128)}, f32[256,2048]{1,0:T(8,128)}, f32[256,2048]{1,0:T(8,128)}), (f32[256,2048]{1,0:T(8,128)}, f32[256,2048]{1,0:T(8,128)}, f32[256,2048]{1,0:T(8,128)}, ...) | async-done | bytes 8388624 | tf_op jit(solution)/shard_map/psum | solution.py:12
  381.8 32.2 %fusion = f32[2048,4096]{1,0:T(8,128)} fusion(f32[256,2048]{1,0:T(8,128)} %get-tuple-element.7, f32[256,2048]{1,0:T(8,128)} %get-tuple-element.8, f32[256,2048]{1,0:T(8,128)S(1)} %copy-done, f32[2048]{0:T(1024)S(1)} %dynamic_slice.10, f32[256]{0:T(256)S(1)} %add_rsqrt_fusion.1), kind=kOutput, calls=%fused_computation.1 | convolution fusion | flops 25771900928 | bytes 39855104 | tf_op jit(solution)/shard_map/dot_general | solution.py:16
  414.0 45.6 %multiply_add_fusion = f32[2048,4096]{1,0:T(8,128)} fusion(f32[2048,4096]{1,0:T(8,128)} %param.9, f32[2048,4096]{1,0:T(8,128)} %fusion, f32[256,2048]{1,0:T(8,128)} %get-tuple-element.9, f32[256,2048]{1,0:T(8,128)} %get-tuple-element.10, f32[256,2048]{1,0:T(8,128)} %get-tuple-element.12, f32[256]{0:T(256)S(1)} %add_rsqrt_fusion, f32[2048]{0:T(1024)S(1)} %dynamic_slice.10), kind=kOutput, calls=%fused_computation | convolution fusion | flops 25797066752 | bytes 106963968 | tf_op jit(solution)/shard_map/dot_general | solution.py:16
  (2 shorter events, 0.0 us)
Async XLA Ops:
  6.5 33.2 %all-gather.7.cloned.1.call-start = ((), (), s32[]{:S(2)}) async-start(), calls=%async_computation.1 | async-start | bytes 2359296 | tf_op jit(solution)/shard_map/all_gather | solution.py:41
  8.4 61.1 %all-gather.5.cloned.1.call-start = ((), (), s32[]{:S(2)}) async-start(), calls=%async_computation | async-start | bytes 2359296 | tf_op jit(solution)/shard_map/all_gather | solution.py:41
  9.2 227.1 %all-reduce.8.cloned.1.call-start = ((), (), s32[]{:S(2)}) async-start(), calls=%async_computation.3 | async-start | bytes 8388608 | tf_op jit(solution)/shard_map/psum | solution.py:48
  48.5 29.7 %copy-start.3 = (f32[2,64,2048]{2,1,0:T(8,128)S(1)}, f32[2,64,2048]{2,1,0:T(8,128)}, u32[]{:S(2)}) copy-start(f32[2,64,2048]{2,1,0:T(8,128)} %param.7) | copy-start | bytes 3145732
  78.4 1.3 copy-start.2
  79.7 1.3 copy-start.1
  81.1 300.7 %all-reduce.6.cloned.1.call-start = ((), (), s32[]{:S(2)}) async-start(), calls=%async_computation.2 | async-start | bytes 16777216 | tf_op jit(solution)/shard_map/psum | solution.py:12
  236.3 16.4 %copy-start = (f32[256,2048]{1,0:T(8,128)S(1)}, f32[256,2048]{1,0:T(8,128)}, u32[]{:S(2)}) copy-start(f32[256,2048]{1,0:T(8,128)} %get-tuple-element.11) | copy-start | bytes 6291460
Sparse Core Ops, SparseCore 0:
  9.2 30.4 all-gather.6
  41.6 27.7 all-gather.4
  81.2 155.0 all-reduce.7
  258.2 123.5 all-reduce.5
where the time goes:
time: 466 us
  waiting for transfers between devices  330 us (71%)
  matrix products  95.2 us (20%)
  blocking collectives  13.6 us (3%)
  between operations  13.2 us (3%)
  other arithmetic  8.37 us (2%)
  local copies, waits for them, and re-layouts  5.2 us (1%)
    psum x1, waiting for transfers between devices, body(): row_panel = lax.psum(partial_value, 'col')  154 us
    psum x1, waiting for transfers between devices, spread(): return lax.psum(block, axis)  124 us
    dot_general x2, matrix products, outer_sum(): lax.dot_general(left_rows, right_rows, (((0,), (0,)), ((), ())), precisio...  77.8 us
    all_gather x2, waiting for transfers between devices, body(): lax.all_gather(attn_out[block_index], 'row', axis=0, tiled=True)  51.5 us
    dot_general x2, matrix products, body(): jnp.dot(lax.all_gather(attn_out[block_index], 'row', axis=0, tiled=True),...  17.4 us
    psum x1, blocking collectives, body(): panel_sums = lax.psum(jnp.sum(row_panel * row_panel, axis=1), 'row')  13.6 us
  transfers between devices with their start and end apart: 4, of which 4 were waited for; matrix products, arithmetic and copies ran while one was open for 2% of the time, Pallas kernels for 0%

commit v1 on v0

--- a/solution.py
+++ b/solution.py
@@ -45,7 +45,12 @@
         offset = col_index * local_tokens
         own_rows = lax.dynamic_slice_in_dim(partial_value, offset, local_tokens, 0) + resid_block
         partial_value = lax.dynamic_update_slice_in_dim(partial_value, own_rows, offset, 0)
-        row_panel = lax.psum(partial_value, "col")
+        chips = jax.lax.axis_size("col")
+        row_panel = partial_value
+        for m in [k for k in (1, 2, 4, 8, 16) if k < chips]:
+            row_panel = row_panel + jax.lax.ppermute(
+                row_panel, "col", tuple(((dev_j, dev_j ^ m) for dev_j in range(chips)))
+            )
         panel_sums = lax.psum(jnp.sum(row_panel * row_panel, axis=1), "row")
         inverse_rms = lax.rsqrt(panel_sums / model_width + epsilon_norm)
         row_panel = row_panel * inverse_rms[:, None] * gain_rows[None, :]

time: 466 us -> 542 us (1.16)
  waiting for transfers between devices: 330 us -> 399 us
  other arithmetic: 8.37 us -> 14.8 us
    ppermute x0 -> x4, waiting for transfers between devices: none -> 221 us  [body(): jax.lax.ppermute(row_panel, 'col', tuple(((dev_j, dev_j ^ m) for dev_j in...]
    psum x1 -> x0, waiting for transfers between devices: 154 us -> none  [body(): row_panel = lax.psum(partial_value, 'col')]
  transfers between devices with their start and end apart: 4 -> 7, of which waited for: 4 -> 7; matrix products, arithmetic and copies ran while one was open for 2% -> 3% of each run, Pallas kernels for 0% -> 0%
where the time goes in v1:
time: 542 us
  waiting for transfers between devices  399 us (74%)
  matrix products  95.2 us (18%)
  other arithmetic  14.8 us (3%)
  between operations  13.2 us (2%)
  blocking collectives  12 us (2%)
    ppermute x4, waiting for transfers between devices, body(): jax.lax.ppermute(row_panel, 'col', tuple(((dev_j, dev_j ^ m) for dev_j in...  221 us
    psum x1, waiting for transfers between devices, spread(): return lax.psum(block, axis)  126 us
    dot_general x2, matrix products, outer_sum(): lax.dot_general(left_rows, right_rows, (((0,), (0,)), ((), ())), precisio...  77.8 us
    all_gather x2, waiting for transfers between devices, body(): lax.all_gather(attn_out[block_index], 'row', axis=0, tiled=True)  51.5 us
    dot_general x2, matrix products, body(): jnp.dot(lax.all_gather(attn_out[block_index], 'row', axis=0, tiled=True),...  17.4 us
    psum x1, blocking collectives, body(): panel_sums = lax.psum(jnp.sum(row_panel * row_panel, axis=1), 'row')  12 us
  transfers between devices with their start and end apart: 7, of which 7 were waited for; matrix products, arithmetic and copies ran while one was open for 3% of the time, Pallas kernels for 0%

profile of v1, /device:TPU:0, one launch (start us, length us, event | category | flops | bytes accessed | tf_op | source)
XLA Modules:
  0.0 541.6 jit_solution(1753046472106324020)
XLA Ops:
  6.5 0.0 all-gather.5.cloned.1.call-start
  6.5 1.8 fusion.23
  8.4 0.0 all-gather.5.cloned.1.call-update
  8.4 0.0 all-gather.7.cloned.1.call-start
  8.5 0.7 all-gather.7.cloned.1.call-update
  9.2 0.0 all-reduce.4.cloned.1.call-start
  9.2 30.5 %all-gather.5.cloned.1.call-done = bf16[1,256,4096]{2,1,0:T(8,128)(2,1)} async-done(((bf16[1,32,4096]{2,1,0:T(8,128)(2,1)}), bf16[1,256,4096]{2,1,0:T(8,128)(2,1)}) %all-gather.5.cloned.1.call-update) | async-done | bytes 2097168 | tf_op jit(solution)/shard_map/all_gather | solution.py:41
  39.8 8.7 %fusion.9 = f32[256,2048]{1,0:T(8,128)S(1)} fusion(bf16[4096,2048]{1,0:T(8,128)(2,1)} %param.6, bf16[1,256,4096]{2,1,0:T(8,128)(2,1)} %all-gather.5.cloned.1.call-done), kind=kOutput, calls=%fused_computation.10 | convolution fusion | flops 4294967296 | bytes 20971520 | tf_op jit(solution)/shard_map/dot_general | solution.py:40
  48.5 0.0 copy-start.1
  48.5 21.0 %all-gather.7.cloned.1.call-done = bf16[1,256,4096]{2,1,0:T(8,128)(2,1)} async-done(((bf16[1,32,4096]{2,1,0:T(8,128)(2,1)}), bf16[1,256,4096]{2,1,0:T(8,128)(2,1)}) %all-gather.7.cloned.1.call-update) | async-done | bytes 2097168 | tf_op jit(solution)/shard_map/all_gather | solution.py:41
  69.5 8.7 %fusion.7 = f32[256,2048]{1,0:T(8,128)S(1)} fusion(bf16[4096,2048]{1,0:T(8,128)(2,1)} %param.6, bf16[1,256,4096]{2,1,0:T(8,128)(2,1)} %all-gather.7.cloned.1.call-done), kind=kOutput, calls=%fused_computation.8 | convolution fusion | flops 4294967296 | bytes 20971520 | tf_op jit(solution)/shard_map/dot_general | solution.py:40
  78.2 0.0 copy-done.1
  78.2 0.2 fusion.20
  78.4 0.0 copy-start
  78.4 1.6 collective-permute-start
  80.0 0.5 collective-permute-start.2
  80.5 0.0 copy-done
  80.5 46.5 %collective-permute-done = f32[256,2048]{1,0:T(8,128)S(1)} collective-permute-done((f32[256,2048]{1,0:T(8,128)S(1)}, f32[256,2048]{1,0:T(8,128)S(1)}, u32[]{:S(2)}, u32[]{:S(2)}) %collective-permute-start) | collective-permute-done | bytes 2097184 | tf_op jit(solution)/shard_map/ppermute | solution.py:51
  127.0 1.9 add.57
  128.9 2.5 collective-permute-start.1
  131.4 81.9 %collective-permute-done.2 = f32[256,2048]{1,0:T(8,128)S(1)} collective-permute-done((f32[256,2048]{1,0:T(8,128)S(1)}, f32[256,2048]{1,0:T(8,128)S(1)}, u32[]{:S(2)}, u32[]{:S(2)}) %collective-permute-start.2) | collective-permute-done | bytes 2097184 | tf_op jit(solution)/shard_map/ppermute | solution.py:51
  213.2 1.7 add.63
  214.9 0.0 collective-permute-start.3
  214.9 0.7 dynamic_slice.10
  215.6 52.8 %collective-permute-done.1 = f32[256,2048]{1,0:T(8,128)} collective-permute-done((f32[256,2048]{1,0:T(8,128)S(1)}, f32[256,2048]{1,0:T(8,128)}, u32[]{:S(2)}, u32[]{:S(2)}) %collective-permute-start.1) | collective-permute-done | bytes 2097184 | tf_op jit(solution)/shard_map/ppermute | solution.py:51
  268.3 3.1 multiply_reduce_fusion.1
  271.5 39.5 %collective-permute-done.3 = f32[256,2048]{1,0:T(8,128)} collective-permute-done((f32[256,2048]{1,0:T(8,128)}, f32[256,2048]{1,0:T(8,128)}, u32[]{:S(2)}, u32[]{:S(2)}) %collective-permute-start.3) | collective-permute-done | bytes 2097184 | tf_op jit(solution)/shard_map/ppermute | solution.py:51
  311.0 2.5 multiply_reduce_fusion
  313.5 12.0 %all-reduce = (f32[256]{0:T(256)S(1)}, f32[256]{0:T(256)S(1)}) all-reduce(f32[256]{0:T(256)S(1)} %get-tuple-element.13, f32[256]{0:T(256)S(1)} %get-tuple-element.11), channel_id=1, replica_groups=mesh['row'=8,'col'=4] {'row'}, use_global_device_ids=true, to_apply=%region_5.6 | all-reduce | flops 512 | bytes 4096 | tf_op jit(solution)/shard_map/psum | solution.py:54
  325.6 5.4 fusion.12
  331.0 0.0 all-reduce.4.cloned.1.call-update
  331.0 126.3 %all-reduce.4.cloned.1.call-done = (f32[256,2048]{1,0:T(8,128)}, f32[256,2048]{1,0:T(8,128)}, f32[256,2048]{1,0:T(8,128)}, f32[256,2048]{1,0:T(8,128)}) async-done(((f32[256,2048]{1,0:T(8,128)}, f32[256,2048]{1,0:T(8,128)}, f32[256,2048]{1,0:T(8,128)}, f32[256,2048]{1,0:T(8,128)}), (f32[256,2048]{1,0:T(8,128)}, f32[256,2048]{1,0:T(8,128)}, f32[256,2048]{1,0:T(8,128)}, ...) | async-done | bytes 8388624 | tf_op jit(solution)/shard_map/psum | solution.py:12
  457.3 32.2 %fusion.3 = f32[2048,4096]{1,0:T(8,128)} fusion(f32[256,2048]{1,0:T(8,128)} %get-tuple-element.7, f32[256,2048]{1,0:T(8,128)} %get-tuple-element.8, f32[256,2048]{1,0:T(8,128)S(1)} %get-tuple-element.14, f32[256]{0:T(256)S(1)} %get-tuple-element.25, f32[2048]{0:T(1024)S(1)} %dynamic_slice.10), kind=kOutput, calls=%fused_computation.4 | convolution fusion | flops 25771900928 | bytes 39855104 | tf_op jit(solution)/shard_map/dot_general | solution.py:16
  489.5 45.6 %multiply_add_fusion = f32[2048,4096]{1,0:T(8,128)} fusion(f32[2048,4096]{1,0:T(8,128)} %param.9, f32[2048,4096]{1,0:T(8,128)} %fusion.3, f32[256,2048]{1,0:T(8,128)} %get-tuple-element.9, f32[256,2048]{1,0:T(8,128)} %get-tuple-element.10, f32[256,2048]{1,0:T(8,128)} %get-tuple-element.12, f32[2048]{0:T(1024)S(1)} %dynamic_slice.10, f32[256]{0:T(256)S(1)} %get-tuple-element.26), kind=kOutput, calls=%fused_computation | convolution fusion | flops 25797066752 | bytes 106963968 | tf_op jit(solution)/shard_map/dot_general | solution.py:16
  (1 shorter events, 0.0 us)
Async XLA Ops:
  6.5 33.2 %all-gather.5.cloned.1.call-start = ((), (), s32[]{:S(2)}) async-start(), calls=%async_computation | async-start | bytes 2359296 | tf_op jit(solution)/shard_map/all_gather | solution.py:41
  8.4 61.1 %all-gather.7.cloned.1.call-start = ((), (), s32[]{:S(2)}) async-start(), calls=%async_computation.1 | async-start | bytes 2359296 | tf_op jit(solution)/shard_map/all_gather | solution.py:41
  9.2 448.1 %all-reduce.4.cloned.1.call-start = ((), (), s32[]{:S(2)}) async-start(), calls=%async_computation.2 | async-start | bytes 16777216 | tf_op jit(solution)/shard_map/psum | solution.py:12
  48.5 29.7 %copy-start.1 = (f32[2,64,2048]{2,1,0:T(8,128)S(1)}, f32[2,64,2048]{2,1,0:T(8,128)}, u32[]{:S(2)}) copy-start(f32[2,64,2048]{2,1,0:T(8,128)} %param.7) | copy-start | bytes 3145732
  78.4 2.1 copy-start
  78.4 48.6 %collective-permute-start = (f32[256,2048]{1,0:T(8,128)S(1)}, f32[256,2048]{1,0:T(8,128)S(1)}, u32[]{:S(2)}, u32[]{:S(2)}) collective-permute-start(f32[256,2048]{1,0:T(8,128)S(1)} %get-tuple-element.19), channel_id=1, source_target_pairs={{0,1},{1,0},{2,3},{3,2},{4,5},{5,4},{6,7},{7,6},{8,9},{9,8},{10,11... | collective-permute-start | bytes 6291464 | tf_op jit(solution)/shard_map/ppermute | solution.py:51
  80.0 133.2 %collective-permute-start.2 = (f32[256,2048]{1,0:T(8,128)S(1)}, f32[256,2048]{1,0:T(8,128)S(1)}, u32[]{:S(2)}, u32[]{:S(2)}) collective-permute-start(f32[256,2048]{1,0:T(8,128)S(1)} %get-tuple-element.20), channel_id=1, source_target_pairs={{0,1},{1,0},{2,3},{3,2},{4,5},{5,4},{6,7},{7,6},{8,9},{9,8},{10,11... | collective-permute-start | bytes 6291464 | tf_op jit(solution)/shard_map/ppermute | solution.py:51
  128.9 139.5 %collective-permute-start.1 = (f32[256,2048]{1,0:T(8,128)S(1)}, f32[256,2048]{1,0:T(8,128)}, u32[]{:S(2)}, u32[]{:S(2)}) collective-permute-start(f32[256,2048]{1,0:T(8,128)S(1)} %add.57), channel_id=1, source_target_pairs={{0,2},{1,3},{2,0},{3,1},{4,6},{5,7},{6,4},{7,5},{8,10},{9,11},{10,... | collective-permute-start | bytes 6291464 | tf_op jit(solution)/shard_map/ppermute | solution.py:51
  214.9 96.1 %collective-permute-start.3 = (f32[256,2048]{1,0:T(8,128)}, f32[256,2048]{1,0:T(8,128)}, u32[]{:S(2)}, u32[]{:S(2)}) collective-permute-start(f32[256,2048]{1,0:T(8,128)} %add.63), channel_id=1, source_target_pairs={{0,2},{1,3},{2,0},{3,1},{4,6},{5,7},{6,4},{7,5},{8,10},{9,11},{10,... | collective-permute-start | bytes 6291464 | tf_op jit(solution)/shard_map/ppermute | solution.py:51
Sparse Core Ops, SparseCore 0:
  9.2 30.4 all-gather.4
  41.6 27.7 all-gather.6
  331.1 126.1 all-reduce.3
